TPU v7x, 32 devices: a whole 2x2x4 slice. The times are simulated.
32 devices in a mesh: dp: 8 (over z, x), tensor: 4 (over y, core).
Axes of the slice: x: 2, y: 2, z: 4, core: 2. Of those that a mesh axis runs over, the one named last changes fastest.
Arguments:
- patches: bfloat16 [192, 50, 1024], P(('dp', 'tensor')), may hold values from -6 to 6
- keep_index: int32 [192, 50], P(('dp', 'tensor')), may hold values from 0 to 49, each once within a row
- kept_count: int32 [192], P(('dp', 'tensor')), may hold values from 25 to 50, as said below
- norm_gain: float32 [2, 2, 1024], replicated, may hold values from 0.5 to 1.5
- shifts: float32 [2, 4, 1024], replicated, may hold values from -3 to 3
- w_qkv: bfloat16 [2, 1024, 3, 1024], P(None, None, None, 'tensor'), may hold values from -0.1875 to 0.1875
- bias_qv: float32 [2, 2, 1024], P(None, None, 'tensor'), may hold values from -3 to 3
- w_out: bfloat16 [2, 1024, 1024], P(None, 'tensor'), may hold values from -1 to 1
- w_fc1: bfloat16 [2, 1024, 4096], P(None, None, 'tensor'), may hold values from -0.1875 to 0.1875
- bias_fc1: float32 [2, 4096], P(None, 'tensor'), may hold values from -3 to 3
- w_fc2: bfloat16 [2, 4096, 1024], P(None, 'tensor'), may hold values from -0.09375 to 0.09375
- cotangent: bfloat16 [192, 50, 1024], P(('dp', 'tensor')), may hold values from -6 to 6
Outputs:
- layer_out: float32 [192, 50, 1024], P(('dp', 'tensor'))
- grad_patches: float32 [192, 50, 1024], P(('dp', 'tensor'))
- grad_gain: float32 [2, 2, 1024], replicated
- grad_shifts: float32 [2, 4, 1024], replicated
- grad_qkv: float32 [2, 1024, 3, 1024], P(None, 'dp', None, 'tensor')
- grad_bias_qv: float32 [2, 2, 1024], replicated
- grad_out: float32 [2, 1024, 1024], P(None, 'tensor', 'dp')
- grad_fc1: float32 [2, 1024, 4096], P(None, 'dp', 'tensor')
- grad_bias_fc1: float32 [2, 4096], replicated
- grad_fc2: float32 [2, 4096, 1024], P(None, 'tensor', 'dp')
Inputs may be any that keep to these rules, and one draw needn't show every extreme that they name: Each row of keep_index holds every patch index once. `kept_count`: some image keeps all 50 slots and some keeps 25.
All inputs are finite; a program needn't handle non-finite values.
Results may differ from a plain program's by a relative error of at most 0.039.
Values may be sent and summed in bfloat16 or wider, within the bound.
A program may use at most 192 MiB of HBM per device.

v0:
```python
from functools import partial
import jax
import jax.numpy as jnp
from jax import lax
from jax.sharding import PartitionSpec as P

D = 1024
HEAD = 64
FF = 4096
LAYERS = 2
PATCHES = 50
EPS = 1e-06
HIGHEST = lax.Precision.HIGHEST


def norm_rows(values, scaling, offset):
    average = jnp.mean(values, axis=-1, keepdims=True)
    centred = values - average
    variance = jnp.mean(centred * centred, axis=-1, keepdims=True)
    return centred * lax.rsqrt(variance + EPS) * scaling + offset


def spread(rows, counts):
    return (
        lax.all_gather(rows, "tensor", axis=0, tiled=True),
        lax.all_gather(counts, "tensor", axis=0, tiled=True),
    )


def collect(partial_rows):
    return lax.psum_scatter(
        partial_rows.astype(jnp.bfloat16), "tensor", scatter_dimension=0, tiled=True
    ).astype(jnp.float32)


def spread_grad(rows):
    return lax.all_gather(rows, "tensor", axis=0, tiled=True)


def collect_grad(partial_rows):
    return lax.psum_scatter(
        partial_rows.astype(jnp.bfloat16), "tensor", scatter_dimension=0, tiled=True
    ).astype(jnp.float32)


def collect_weight(partial_grad, split_dim):
    return lax.psum_scatter(
        partial_grad.astype(jnp.bfloat16), "dp", scatter_dimension=split_dim, tiled=True
    ).astype(jnp.float32)


def score_block(queries, key_rows, visible, score_scale):
    scores = (
        jnp.einsum("bqhe,bkhe->bhqk", queries, key_rows, preferred_element_type=jnp.float32)
        * score_scale
    )
    return jnp.where(visible[:, None, None, :], scores, -1e30)


def local(
    patches,
    keep_index,
    kept_count,
    norm_gain,
    shifts,
    w_qkv,
    bias_qv,
    w_out,
    w_fc1,
    bias_fc1,
    w_fc2,
    cotangent,
):
    width_local = w_qkv.shape[-1]
    hidden_local = w_fc1.shape[-1]
    heads_local = width_local // HEAD
    score_scale = HEAD ** (-0.5)
    slot_ids = jnp.arange(PATCHES, dtype=jnp.int32)
    selector = (keep_index[:, :, None] == slot_ids[None, None, :]).astype(jnp.bfloat16)
    residual = jnp.einsum("bsp,bpd->bsd", selector, patches, preferred_element_type=jnp.float32)
    stored = []
    visible = None
    shape_heads = None
    image_total = 0
    for layer_no in range(LAYERS):
        normed_own = norm_rows(residual, norm_gain[layer_no, 0], shifts[layer_no, 0]).astype(
            jnp.bfloat16
        )
        normed, counts_all = spread(normed_own, kept_count)
        visible = slot_ids[None, :] < counts_all[:, None]
        image_total = normed.shape[0]
        shape_heads = (image_total, PATCHES, heads_local, HEAD)
        triple = jnp.einsum(
            "bsd,dce->bsce", normed, w_qkv[layer_no], preferred_element_type=jnp.float32
        )
        queries = (triple[:, :, 0] + bias_qv[layer_no, 0]).astype(jnp.bfloat16).reshape(shape_heads)
        key_rows = triple[:, :, 1].astype(jnp.bfloat16).reshape(shape_heads)
        value_rows = (
            (triple[:, :, 2] + bias_qv[layer_no, 1]).astype(jnp.bfloat16).reshape(shape_heads)
        )
        scores = score_block(queries, key_rows, visible, score_scale)
        log_total = jax.nn.logsumexp(scores, axis=-1, keepdims=True)
        attn_weights = jnp.exp(scores - log_total).astype(jnp.bfloat16)
        attended = jnp.einsum(
            "bhqk,bkhe->bqhe", attn_weights, value_rows, preferred_element_type=jnp.float32
        )
        attended = attended.reshape(image_total, PATCHES, width_local).astype(jnp.bfloat16)
        mixed = collect(
            jnp.einsum("bse,ed->bsd", attended, w_out[layer_no], preferred_element_type=jnp.float32)
        )
        middle = residual + mixed + shifts[layer_no, 2]
        normed_mid = norm_rows(middle, norm_gain[layer_no, 1], shifts[layer_no, 1]).astype(
            jnp.bfloat16
        )
        normed_mlp, counts_again = spread(normed_mid, kept_count)
        pre_act = (
            jnp.einsum(
                "bsd,df->bsf", normed_mlp, w_fc1[layer_no], preferred_element_type=jnp.float32
            )
            + bias_fc1[layer_no]
        )
        activated = jax.nn.gelu(pre_act, approximate=False).astype(jnp.bfloat16)
        stored.append(
            (
                residual,
                normed,
                queries,
                key_rows,
                value_rows,
                log_total,
                attended,
                middle,
                normed_mlp,
                pre_act,
                activated,
            )
        )
        mlp_part = collect(
            jnp.einsum(
                "bsf,fd->bsd", activated, w_fc2[layer_no], preferred_element_type=jnp.float32
            )
        )
        residual = middle + mlp_part + shifts[layer_no, 3]
    own_mask = (slot_ids[None, :] < kept_count[:, None]).astype(jnp.float32)[:, :, None]
    layer_out = residual * own_mask
    gradient = cotangent.astype(jnp.float32) * own_mask
    offset_at = lax.axis_index("tensor") * width_local
    hidden_at = lax.axis_index("tensor") * hidden_local
    gain_terms = []
    shift_terms = []
    bias_qv_terms = []
    bias_fc1_terms = []
    weight_terms = []
    for layer_no in reversed(range(LAYERS)):
        (
            residual_in,
            normed,
            queries,
            key_rows,
            value_rows,
            log_total,
            attended,
            middle,
            normed_mlp,
            pre_act,
            activated,
        ) = stored[layer_no]
        grad_mlp = gradient.astype(jnp.bfloat16)
        shift_fc2 = jnp.sum(grad_mlp.astype(jnp.float32), axis=(0, 1))
        grad_rows = spread_grad(grad_mlp)
        d_fc2 = jnp.einsum("bsf,bsd->fd", activated, grad_rows, preferred_element_type=jnp.float32)
        d_act = jnp.einsum(
            "bsd,fd->bsf", grad_rows, w_fc2[layer_no], preferred_element_type=jnp.float32
        )
        gelu_pull = jax.vjp(partial(jax.nn.gelu, approximate=False), pre_act)[1]
        d_pre = gelu_pull(d_act)[0].astype(jnp.bfloat16)
        d_bias_fc1 = jnp.sum(d_pre.astype(jnp.float32), axis=(0, 1))
        d_fc1 = jnp.einsum("bsd,bsf->df", normed_mlp, d_pre, preferred_element_type=jnp.float32)
        d_normed = collect_grad(
            jnp.einsum("bsf,df->bsd", d_pre, w_fc1[layer_no], preferred_element_type=jnp.float32)
        )
        norm_pull = jax.vjp(norm_rows, middle, norm_gain[layer_no, 1], shifts[layer_no, 1])[1]
        d_middle, d_gain_mlp, d_shift_mlp = norm_pull(d_normed)
        gradient = gradient + d_middle
        grad_attn = gradient.astype(jnp.bfloat16)
        shift_attn = jnp.sum(grad_attn.astype(jnp.float32), axis=(0, 1))
        grad_rows = spread_grad(grad_attn)
        d_out = jnp.einsum("bse,bsd->ed", attended, grad_rows, preferred_element_type=jnp.float32)
        d_attended = jnp.einsum(
            "bsd,ed->bse", grad_rows, w_out[layer_no], preferred_element_type=jnp.float32
        )
        d_attended = d_attended.astype(jnp.bfloat16).reshape(shape_heads)
        scores = score_block(queries, key_rows, visible, score_scale)
        probability = jnp.exp(scores - log_total)
        d_values = jnp.einsum(
            "bhqk,bqhe->bkhe",
            probability.astype(jnp.bfloat16),
            d_attended,
            preferred_element_type=jnp.float32,
        )
        d_prob = jnp.einsum(
            "bqhe,bkhe->bhqk", d_attended, value_rows, preferred_element_type=jnp.float32
        )
        centre_term = jnp.sum(probability * d_prob, axis=-1, keepdims=True)
        d_scores = (probability * (d_prob - centre_term)).astype(jnp.bfloat16)
        d_queries = (
            jnp.einsum("bhqk,bkhe->bqhe", d_scores, key_rows, preferred_element_type=jnp.float32)
            * score_scale
        )
        d_keys = (
            jnp.einsum("bhqk,bqhe->bkhe", d_scores, queries, preferred_element_type=jnp.float32)
            * score_scale
        )
        d_triple = jnp.stack([d_queries, d_keys, d_values], axis=2)
        d_triple = d_triple.reshape(image_total, PATCHES, 3, width_local).astype(jnp.bfloat16)
        d_bias_qv = jnp.sum(d_triple[:, :, 0::2].astype(jnp.float32), axis=(0, 1))
        d_qkv = jnp.einsum("bsd,bsce->dce", normed, d_triple, preferred_element_type=jnp.float32)
        d_normed = collect_grad(
            jnp.einsum(
                "bsce,dce->bsd", d_triple, w_qkv[layer_no], preferred_element_type=jnp.float32
            )
        )
        norm_pull = jax.vjp(norm_rows, residual_in, norm_gain[layer_no, 0], shifts[layer_no, 0])[1]
        d_input, d_gain_attn, d_shift_attn = norm_pull(d_normed)
        gradient = gradient + d_input
        gain_terms.insert(0, jnp.stack([d_gain_attn, d_gain_mlp]))
        shift_terms.insert(0, jnp.stack([d_shift_attn, d_shift_mlp, shift_attn, shift_fc2]))
        bias_qv_terms.insert(0, d_bias_qv)
        bias_fc1_terms.insert(0, d_bias_fc1)
        weight_terms.insert(
            0,
            (
                collect_weight(d_qkv, 0),
                collect_weight(d_out, 1),
                collect_weight(d_fc1, 0),
                collect_weight(d_fc2, 1),
            ),
        )
    grad_qkv, grad_out, grad_fc1, grad_fc2 = (
        jnp.stack([entry[k] for entry in weight_terms]) for k in range(4)
    )
    zero_at = offset_at * 0
    qv_full = lax.dynamic_update_slice(
        jnp.zeros((LAYERS, 2, D), jnp.float32),
        jnp.stack(bias_qv_terms),
        (zero_at, zero_at, offset_at),
    )
    fc1_full = lax.dynamic_update_slice(
        jnp.zeros((LAYERS, FF), jnp.float32), jnp.stack(bias_fc1_terms), (zero_at, hidden_at)
    )
    grad_gain, grad_shifts, grad_bias_qv, grad_bias_fc1 = lax.psum(
        (jnp.stack(gain_terms), jnp.stack(shift_terms), qv_full, fc1_full), ("dp", "tensor")
    )
    grad_patches = jnp.einsum(
        "bsp,bsd->bpd", selector.astype(jnp.float32), gradient, precision=HIGHEST
    )
    return (
        layer_out,
        grad_patches,
        grad_gain,
        grad_shifts,
        grad_qkv,
        grad_bias_qv,
        grad_out,
        grad_fc1,
        grad_bias_fc1,
        grad_fc2,
    )


def solution(mesh):
    in_specs = (
        P(("dp", "tensor"), None, None),
        P(("dp", "tensor"), None),
        P(("dp", "tensor")),
        P(),
        P(),
        P(None, None, None, "tensor"),
        P(None, None, "tensor"),
        P(None, "tensor", None),
        P(None, None, "tensor"),
        P(None, "tensor"),
        P(None, "tensor", None),
        P(("dp", "tensor"), None, None),
    )
    out_specs = (
        P(("dp", "tensor"), None, None),
        P(("dp", "tensor"), None, None),
        P(),
        P(),
        P(None, "dp", None, "tensor"),
        P(),
        P(None, "tensor", "dp"),
        P(None, "dp", "tensor"),
        P(),
        P(None, "tensor", "dp"),
    )
    return jax.shard_map(local, mesh=mesh, in_specs=in_specs, out_specs=out_specs, check_vma=False)
```

profile of v0, /device:TPU:8, one launch (start us, length us, event | category | flops | bytes accessed | tf_op | source)
XLA Modules:
  0.0 1404.0 jit_solution(15501463727336067155)
XLA Ops:
  13.6 4.9 all-reduce
  18.6 20.9 %all-gather.9.cloned.1.call-done = bf16[24,50,1024]{2,1,0:T(8,128)(2,1)} async-done(((bf16[6,50,1024]{2,1,0:T(8,128)(2,1)}), bf16[24,50,1024]{2,1,0:T(8,128)(2,1)}) %all-gather.9.cloned.1.call-update) | async-done | bytes 2457616 | tf_op jit(solution)/shard_map/all_gather | solution.py:25
  39.5 4.6 fusion.18
  68.2 35.5 %reduce-scatter.25.cloned.1.call-done = bf16[6,50,1024]{2,1,0:T(8,128)(2,1)} async-done(((bf16[24,50,1024]{2,1,0:T(8,128)(2,1)}), bf16[6,50,1024]{2,1,0:T(8,128)(2,1)}) %reduce-scatter.25.cloned.1.call-update) | async-done | bytes 614416 | tf_op jit(solution)/shard_map/reduce_scatter | solution.py:31
  107.4 25.6 %all-gather.11.cloned.1.call-done = bf16[24,50,1024]{2,1,0:T(8,128)(2,1)} async-done(((bf16[6,50,1024]{2,1,0:T(8,128)(2,1)}), bf16[24,50,1024]{2,1,0:T(8,128)(2,1)}) %all-gather.11.cloned.1.call-update) | async-done | bytes 2457616 | tf_op jit(solution)/shard_map/all_gather | solution.py:25
  133.1 7.1 convert_reduce_fusion.3
  140.2 13.3 multiply_convert_fusion.1
  155.0 4.4 convolution_convert_fusion.5
  159.5 35.6 %reduce-scatter.27.cloned.1.call-done = bf16[6,50,1024]{2,1,0:T(8,128)(2,1)} async-done(((bf16[24,50,1024]{2,1,0:T(8,128)(2,1)}), bf16[6,50,1024]{2,1,0:T(8,128)(2,1)}) %reduce-scatter.27.cloned.1.call-update) | async-done | bytes 614416 | tf_op jit(solution)/shard_map/reduce_scatter | solution.py:31
  198.3 26.0 %all-gather.13.cloned.1.call-done = bf16[24,50,1024]{2,1,0:T(8,128)(2,1)} async-done(((bf16[6,50,1024]{2,1,0:T(8,128)(2,1)}), bf16[24,50,1024]{2,1,0:T(8,128)(2,1)}) %all-gather.13.cloned.1.call-update) | async-done | bytes 2457616 | tf_op jit(solution)/shard_map/all_gather | solution.py:25
  224.4 4.6 fusion.14
  259.7 35.6 %reduce-scatter.29.cloned.1.call-done = bf16[6,50,1024]{2,1,0:T(8,128)(2,1)} async-done(((bf16[24,50,1024]{2,1,0:T(8,128)(2,1)}), bf16[6,50,1024]{2,1,0:T(8,128)(2,1)}) %reduce-scatter.29.cloned.1.call-update) | async-done | bytes 614416 | tf_op jit(solution)/shard_map/reduce_scatter | solution.py:31
  301.9 23.5 %all-gather.15.cloned.1.call-done = bf16[24,50,1024]{2,1,0:T(8,128)(2,1)} async-done(((bf16[6,50,1024]{2,1,0:T(8,128)(2,1)}), bf16[24,50,1024]{2,1,0:T(8,128)(2,1)}) %all-gather.15.cloned.1.call-update) | async-done | bytes 2457616 | tf_op jit(solution)/shard_map/all_gather | solution.py:25
  325.4 7.1 convert_reduce_fusion.1
  334.8 13.5 multiply_convert_fusion
  348.4 5.6 all-gather.17.cloned.1.call-done
  353.9 11.3 convert_reduce_fusion.4
  366.9 4.4 convolution_convert_fusion.3
  371.5 35.4 %reduce-scatter.33.cloned.1.call-done = bf16[6,50,1024]{2,1,0:T(8,128)(2,1)} async-done(((bf16[24,50,1024]{2,1,0:T(8,128)(2,1)}), bf16[6,50,1024]{2,1,0:T(8,128)(2,1)}) %reduce-scatter.33.cloned.1.call-update) | async-done | bytes 614416 | tf_op jit(solution)/shard_map/reduce_scatter | solution.py:41
  415.4 26.4 %all-gather.19.cloned.1.call-done = bf16[24,50,1024]{2,1,0:T(8,128)(2,1)} async-done(((bf16[6,50,1024]{2,1,0:T(8,128)(2,1)}), bf16[24,50,1024]{2,1,0:T(8,128)(2,1)}) %all-gather.19.cloned.1.call-update) | async-done | bytes 2457616 | tf_op jit(solution)/shard_map/all_gather | solution.py:37
  480.0 3.9 bitcast_convert_fusion.1
  484.0 7.0 convolution_convert_fusion.4
  491.1 28.5 %reduce-scatter.35.cloned.1.call-done = bf16[6,50,1024]{2,1,0:T(8,128)(2,1)} async-done(((bf16[24,50,1024]{2,1,0:T(8,128)(2,1)}), bf16[6,50,1024]{2,1,0:T(8,128)(2,1)}) %reduce-scatter.35.cloned.1.call-update) | async-done | bytes 614416 | tf_op jit(solution)/shard_map/reduce_scatter | solution.py:41
  524.1 33.6 %reduce-scatter.31.cloned.1.call-done = bf16[6,50,1024]{2,1,0:T(8,128)(2,1)} async-done(((bf16[24,50,1024]{2,1,0:T(8,128)(2,1)}), bf16[6,50,1024]{2,1,0:T(8,128)(2,1)}) %reduce-scatter.31.cloned.1.call-update) | async-done | bytes 614416 | tf_op jit(solution)/shard_map/reduce_scatter | solution.py:31
  557.7 4.6 convert_reduce_fusion.14
  562.3 26.4 %all-gather.21.cloned.1.call-done = bf16[24,50,1024]{2,1,0:T(8,128)(2,1)} async-done(((bf16[6,50,1024]{2,1,0:T(8,128)(2,1)}), bf16[24,50,1024]{2,1,0:T(8,128)(2,1)}) %all-gather.21.cloned.1.call-update) | async-done | bytes 2457616 | tf_op jit(solution)/shard_map/all_gather | solution.py:37
  588.7 11.3 convert_reduce_fusion.5
  601.6 4.8 convolution_convert_fusion.2
  606.5 35.5 %reduce-scatter.37.cloned.1.call-done = bf16[6,50,1024]{2,1,0:T(8,128)(2,1)} async-done(((bf16[24,50,1024]{2,1,0:T(8,128)(2,1)}), bf16[6,50,1024]{2,1,0:T(8,128)(2,1)}) %reduce-scatter.37.cloned.1.call-update) | async-done | bytes 614416 | tf_op jit(solution)/shard_map/reduce_scatter | solution.py:41
  648.7 6.1 bitcast_convert_fusion.2
  657.5 4.6 fusion.92
  664.2 6.5 bitcast_convert_fusion.3
  670.7 3.9 copy.160
  674.9 7.5 bitcast_convert_fusion.4
  682.5 6.5 bitcast_convert_fusion.5
  694.0 5.6 bitcast_convert_fusion.6
  731.0 6.1 bitcast_convert_fusion
  737.2 8.9 reduce-scatter.55.cloned.1.call-done
  747.5 64.3 %reduce-scatter.51.cloned.1.call-done = bf16[128,256]{1,0:T(8,128)(2,1)} async-done(((bf16[1024,256]{1,0:T(8,128)(2,1)}), bf16[128,256]{1,0:T(8,128)(2,1)}) %reduce-scatter.51.cloned.1.call-update) | async-done | bytes 65552
  812.8 68.6 %reduce-scatter.53.cloned.1.call-done = bf16[128,1024]{1,0:T(8,128)(2,1)} async-done(((bf16[1024,1024]{1,0:T(8,128)(2,1)}), bf16[128,1024]{1,0:T(8,128)(2,1)}) %reduce-scatter.53.cloned.1.call-update) | async-done | bytes 262160
  883.5 68.2 %reduce-scatter.47.cloned.1.call-done = bf16[128,1024]{1,0:T(8,128)(2,1)} async-done(((bf16[1024,1024]{1,0:T(8,128)(2,1)}), bf16[128,1024]{1,0:T(8,128)(2,1)}) %reduce-scatter.47.cloned.1.call-update) | async-done | bytes 262160 | tf_op jit(solution)/shard_map/reduce_scatter | solution.py:47
  951.7 70.2 %reduce-scatter.45.cloned.1.call-done = bf16[128,1024]{1,0:T(8,128)(2,1)} async-done(((bf16[1024,1024]{1,0:T(8,128)(2,1)}), bf16[128,1024]{1,0:T(8,128)(2,1)}) %reduce-scatter.45.cloned.1.call-update) | async-done | bytes 262160 | tf_op jit(solution)/shard_map/reduce_scatter | solution.py:47
  1025.6 61.1 %reduce-scatter.49.cloned.1.call-done = bf16[128,256]{1,0:T(8,128)(2,1)} async-done(((bf16[1024,256]{1,0:T(8,128)(2,1)}), bf16[128,256]{1,0:T(8,128)(2,1)}) %reduce-scatter.49.cloned.1.call-update) | async-done | bytes 65552
  1088.5 66.3 %reduce-scatter.43.cloned.1.call-done = bf16[128,3,256]{2,0,1:T(8,128)(2,1)} async-done(((bf16[1024,3,256]{2,0,1:T(8,128)(2,1)}), bf16[128,3,256]{2,0,1:T(8,128)(2,1)}) %reduce-scatter.43.cloned.1.call-update) | async-done | bytes 196624 | tf_op jit(solution)/shard_map/reduce_scatter | solution.py:47
  1154.8 68.0 %reduce-scatter.41.cloned.1.call-done = bf16[128,3,256]{2,0,1:T(8,128)(2,1)} async-done(((bf16[1024,3,256]{2,0,1:T(8,128)(2,1)}), bf16[128,3,256]{2,0,1:T(8,128)(2,1)}) %reduce-scatter.41.cloned.1.call-update) | async-done | bytes 196624 | tf_op jit(solution)/shard_map/reduce_scatter | solution.py:47
  1224.9 35.4 %reduce-scatter.39.cloned.1.call-done = bf16[6,50,1024]{2,1,0:T(8,128)(2,1)} async-done(((bf16[24,50,1024]{2,1,0:T(8,128)(2,1)}), bf16[6,50,1024]{2,1,0:T(8,128)(2,1)}) %reduce-scatter.39.cloned.1.call-update) | async-done | bytes 614416 | tf_op jit(solution)/shard_map/reduce_scatter | solution.py:41
  1265.1 4.6 fusion.82
  1269.8 121.8 %all-reduce.4.cloned.1.call-done = (f32[2,2,1024]{2,1,0:T(2,128)}, f32[2,4,1024]{2,1,0:T(4,128)}, f32[2,2,1024]{2,1,0:T(2,128)}, f32[2,4096]{1,0:T(2,128)}) async-done(((f32[2,2,1024]{2,1,0:T(2,128)}, f32[2,4,1024]{2,1,0:T(4,128)}, f32[2,2,1024]{2,1,0:T(2,128)}, f32[2,4096]{1,0:T(2,128)}), (f32[2,2,1024]{2,1,0:T(2,128)}, f32[2,4,1024]{2,1,0:T(4,128)}, f32[2,2,1024]{2,1,0:T(2,128)}, ...) | async-done | bytes 98320 | tf_op jit(solution)/shard_map/psum | solution.py:251
  (396 shorter events, 202.2 us)
Async XLA Ops:
  7.2 32.2 %all-gather.9.cloned.1.call-start = ((), (), s32[]{:S(2)}) async-start(), calls=%async_computation.16 | async-start | bytes 3440640 | tf_op jit(solution)/shard_map/all_gather | solution.py:25
  9.5 94.2 %copy-start.4 = (f32[6,50,1024]{2,1,0:T(8,128)}, f32[6,50,1024]{2,1,0:T(8,128)S(1)}, u32[]{:S(2)}) copy-start(f32[6,50,1024]{2,1,0:T(8,128)S(1)} %get-tuple-element.77) | copy-start | bytes 3686404
  10.7 635.9 %copy-start.54 = (f32[1,1,1024]{2,1,0:T(1,128)}, f32[1,1,1024]{2,1,0:T(1,128)S(1)}, u32[]{:S(2)}) copy-start(f32[1,1,1024]{2,1,0:T(1,128)S(1)} %get-tuple-element.71) | copy-start | bytes 12292
  11.8 91.9 %reduce-scatter.25.cloned.1.call-start = ((), (), s32[]{:S(2)}) async-start(), calls=%async_computation.17 | async-start | bytes 3440640 | tf_op jit(solution)/shard_map/reduce_scatter | solution.py:31
  68.1 64.9 %all-gather.11.cloned.1.call-start = ((), (), s32[]{:S(2)}) async-start(), calls=%async_computation.18 | async-start | bytes 3440640 | tf_op jit(solution)/shard_map/all_gather | solution.py:25
  105.1 541.5 %copy-start.2 = (f32[6,50,1024]{2,1,0:T(8,128)}, f32[6,50,1024]{2,1,0:T(8,128)S(1)}, u32[]{:S(2)}) copy-start(f32[6,50,1024]{2,1,0:T(8,128)S(1)} %get-tuple-element.56) | copy-start | bytes 3686404
  105.1 541.5 %copy-start.50 = (f32[6,50]{1,0:T(8,128)}, f32[6,50]{1,0:T(8,128)S(1)}, u32[]{:S(2)}) copy-start(f32[6,50]{1,0:T(8,128)S(1)} %broadcast_multiply_fusion.2) | copy-start | bytes 3604
  105.4 541.2 %copy-start.59 = (f32[6,50]{1,0:T(8,128)}, f32[6,50]{1,0:T(8,128)S(1)}, u32[]{:S(2)}) copy-start(f32[6,50]{1,0:T(8,128)S(1)} %fusion.142) | copy-start | bytes 3604
  106.6 88.5 %reduce-scatter.27.cloned.1.call-start = ((), (), s32[]{:S(2)}) async-start(), calls=%async_computation.19 | async-start | bytes 3440640 | tf_op jit(solution)/shard_map/reduce_scatter | solution.py:31
  159.4 64.9 %all-gather.13.cloned.1.call-start = ((), (), s32[]{:S(2)}) async-start(), calls=%async_computation.20 | async-start | bytes 3440640 | tf_op jit(solution)/shard_map/all_gather | solution.py:25
  197.9 97.4 %reduce-scatter.29.cloned.1.call-start = ((), (), s32[]{:S(2)}) async-start(), calls=%async_computation.21 | async-start | bytes 3440640 | tf_op jit(solution)/shard_map/reduce_scatter | solution.py:31
  259.7 65.7 %all-gather.15.cloned.1.call-start = ((), (), s32[]{:S(2)}) async-start(), calls=%async_computation.22 | async-start | bytes 3440640 | tf_op jit(solution)/shard_map/all_gather | solution.py:25
  298.9 55.0 %all-gather.17.cloned.1.call-start = ((), (), s32[]{:S(2)}) async-start(), calls=%async_computation.24 | async-start | bytes 3440640 | tf_op jit(solution)/shard_map/all_gather | solution.py:37
  301.4 105.6 %reduce-scatter.33.cloned.1.call-start = ((), (), s32[]{:S(2)}) async-start(), calls=%async_computation.25 | async-start | bytes 3440640 | tf_op jit(solution)/shard_map/reduce_scatter | solution.py:41
  371.3 70.5 %all-gather.19.cloned.1.call-start = ((), (), s32[]{:S(2)}) async-start(), calls=%async_computation.26 | async-start | bytes 3440640 | tf_op jit(solution)/shard_map/all_gather | solution.py:37
  415.3 104.3 %reduce-scatter.35.cloned.1.call-start = ((), (), s32[]{:S(2)}) async-start(), calls=%async_computation.27 | async-start | bytes 3440640 | tf_op jit(solution)/shard_map/reduce_scatter | solution.py:41
  484.0 73.7 %reduce-scatter.31.cloned.1.call-start = ((), (), s32[]{:S(2)}) async-start(), calls=%async_computation.23 | async-start | bytes 3440640 | tf_op jit(solution)/shard_map/reduce_scatter | solution.py:31
  491.1 97.6 %all-gather.21.cloned.1.call-start = ((), (), s32[]{:S(2)}) async-start(), calls=%async_computation.28 | async-start | bytes 3440640 | tf_op jit(solution)/shard_map/all_gather | solution.py:37
  562.2 79.8 %reduce-scatter.37.cloned.1.call-start = ((), (), s32[]{:S(2)}) async-start(), calls=%async_computation.29 | async-start | bytes 3440640 | tf_op jit(solution)/shard_map/reduce_scatter | solution.py:41
  606.4 82.7 %all-gather.23.cloned.1.call-start = ((), (), s32[]{:S(2)}) async-start(), calls=%async_computation.30 | async-start | bytes 3440640 | tf_op jit(solution)/shard_map/all_gather | solution.py:37
  648.7 97.4 %reduce-scatter.55.cloned.1.call-start = ((), (), s32[]{:S(2)}) async-start(), calls=%async_computation.39 | async-start | bytes 2359296
  657.4 154.3 %reduce-scatter.51.cloned.1.call-start = ((), (), s32[]{:S(2)}) async-start(), calls=%async_computation.37 | async-start | bytes 589824
  664.2 217.2 %reduce-scatter.53.cloned.1.call-start = ((), (), s32[]{:S(2)}) async-start(), calls=%async_computation.38 | async-start | bytes 2359296
  674.7 277.0 %reduce-scatter.47.cloned.1.call-start = ((), (), s32[]{:S(2)}) async-start(), calls=%async_computation.35 | async-start | bytes 2359296 | tf_op jit(solution)/shard_map/reduce_scatter | solution.py:47
  682.5 339.5 %reduce-scatter.45.cloned.1.call-start = ((), (), s32[]{:S(2)}) async-start(), calls=%async_computation.34 | async-start | bytes 2359296 | tf_op jit(solution)/shard_map/reduce_scatter | solution.py:47
  689.1 397.7 %reduce-scatter.49.cloned.1.call-start = ((), (), s32[]{:S(2)}) async-start(), calls=%async_computation.36 | async-start | bytes 589824
  694.0 460.8 %reduce-scatter.43.cloned.1.call-start = ((), (), s32[]{:S(2)}) async-start(), calls=%async_computation.33 | async-start | bytes 1769472 | tf_op jit(solution)/shard_map/reduce_scatter | solution.py:47
  699.7 523.1 %reduce-scatter.41.cloned.1.call-start = ((), (), s32[]{:S(2)}) async-start(), calls=%async_computation.32 | async-start | bytes 1769472 | tf_op jit(solution)/shard_map/reduce_scatter | solution.py:47
  730.7 529.6 %reduce-scatter.39.cloned.1.call-start = ((), (), s32[]{:S(2)}) async-start(), calls=%async_computation.31 | async-start | bytes 3440640 | tf_op jit(solution)/shard_map/reduce_scatter | solution.py:41
  737.1 75.6 %copy-start.88 = (f32[1024]{0:T(1024)S(1)}, f32[1024]{0:T(1024)}, u32[]{:S(2)}) copy-start(f32[1024]{0:T(1024)} %get-tuple-element.88) | copy-start | bytes 12292
  737.1 75.6 %copy-start.89 = (f32[1024]{0:T(1024)S(1)}, f32[1024]{0:T(1024)}, u32[]{:S(2)}) copy-start(f32[1024]{0:T(1024)} %get-tuple-element.90) | copy-start | bytes 12292
  737.2 654.4 %all-reduce.4.cloned.1.call-start = ((), (), s32[]{:S(2)}) async-start(), calls=%async_computation.40 | async-start | bytes 196608 | tf_op jit(solution)/shard_map/psum | solution.py:251
  812.8 275.7 %copy-start.56 = (f32[2,4096]{1,0:T(2,128)}, f32[2,4096]{1,0:T(2,128)S(1)}, u32[]{:S(2)}) copy-start(f32[2,4096]{1,0:T(2,128)S(1)} %maximum_dynamic-update-slice_fusion) | copy-start | bytes 98308
  882.5 377.8 %copy-start.5 = (f32[6,50,1024]{2,1,0:T(8,128)S(1)}, f32[6,50,1024]{2,1,0:T(8,128)}, u32[]{:S(2)}) copy-start(f32[6,50,1024]{2,1,0:T(8,128)} %copy-done.4) | copy-start | bytes 3686404
  882.5 377.8 %copy-start.53 = (f32[6,50]{1,0:T(8,128)S(1)}, f32[6,50]{1,0:T(8,128)}, u32[]{:S(2)}) copy-start(f32[6,50]{1,0:T(8,128)} %copy-done.52) | copy-start | bytes 3604
  882.5 377.8 %copy-start.58 = (f32[1,1,1024]{2,1,0:T(1,128)S(1)}, f32[1,1,1024]{2,1,0:T(1,128)}, u32[]{:S(2)}) copy-start(f32[1,1,1024]{2,1,0:T(1,128)} %copy-done.57) | copy-start | bytes 12292
  1024.0 237.8 %copy-start.67 = (f32[6,50]{1,0:T(8,128)S(1)}, f32[6,50]{1,0:T(8,128)}, u32[]{:S(2)}) copy-start(f32[6,50]{1,0:T(8,128)} %copy-done.66) | copy-start | bytes 3604
  1024.0 237.8 %copy-start.62 = (f32[6,50]{1,0:T(8,128)S(1)}, f32[6,50]{1,0:T(8,128)}, u32[]{:S(2)}) copy-start(f32[6,50]{1,0:T(8,128)} %copy-done.61) | copy-start | bytes 3604
  1025.6 238.0 %copy-start.63 = (f32[2,2,1024]{2,1,0:T(2,128)}, f32[2,2,1024]{2,1,0:T(2,128)S(1)}, u32[]{:S(2)}) copy-start(f32[2,2,1024]{2,1,0:T(2,128)S(1)} %maximum_dynamic-update-slice_fusion.1) | copy-start | bytes 49156
  1088.5 175.2 %copy-start.72 = (f32[1024]{0:T(1024)S(1)}, f32[1024]{0:T(1024)}, u32[]{:S(2)}) copy-start(f32[1024]{0:T(1024)} %get-tuple-element.45) | copy-start | bytes 12292
  1088.5 175.2 %copy-start.73 = (f32[1024]{0:T(1024)S(1)}, f32[1024]{0:T(1024)}, u32[]{:S(2)}) copy-start(f32[1024]{0:T(1024)} %get-tuple-element.28) | copy-start | bytes 12292
  1088.5 175.2 %copy-start.74 = (f32[1024]{0:T(1024)S(1)}, f32[1024]{0:T(1024)}, u32[]{:S(2)}) copy-start(f32[1024]{0:T(1024)} %get-tuple-element.43) | copy-start | bytes 12292
  1088.5 175.2 %copy-start.75 = (f32[1024]{0:T(1024)S(1)}, f32[1024]{0:T(1024)}, u32[]{:S(2)}) copy-start(f32[1024]{0:T(1024)} %get-tuple-element.26) | copy-start | bytes 12292
  1088.5 175.2 %copy-start.76 = (f32[1024]{0:T(1024)S(1)}, f32[1024]{0:T(1024)}, u32[]{:S(2)}) copy-start(f32[1024]{0:T(1024)} %get-tuple-element.40) | copy-start | bytes 12292
  1088.5 175.2 %copy-start.77 = (f32[1024]{0:T(1024)S(1)}, f32[1024]{0:T(1024)}, u32[]{:S(2)}) copy-start(f32[1024]{0:T(1024)} %get-tuple-element.24) | copy-start | bytes 12292
  1088.5 175.2 %copy-start.82 = (f32[1024]{0:T(1024)S(1)}, f32[1024]{0:T(1024)}, u32[]{:S(2)}) copy-start(f32[1024]{0:T(1024)} %get-tuple-element.38) | copy-start | bytes 12292
  1222.8 42.3 %copy-start.55 = (f32[1,1,1024]{2,1,0:T(1,128)S(1)}, f32[1,1,1024]{2,1,0:T(1,128)}, u32[]{:S(2)}) copy-start(f32[1,1,1024]{2,1,0:T(1,128)} %copy-done.54) | copy-start | bytes 12292
  1265.1 131.9 %copy-start.1 = (bf16[6,50,1024]{2,1,0:T(8,128)(2,1)S(1)}, bf16[6,50,1024]{2,1,0:T(8,128)(2,1)}, u32[]{:S(2)}) copy-start(bf16[6,50,1024]{2,1,0:T(8,128)(2,1)} %param.12) | copy-start | bytes 1843204
  (77 other events, 837.6 us)
Sparse Core Ops, SparseCore 0:
  12.0 27.4 all-gather.8
  68.3 35.4 reduce-scatter.24
  106.7 26.2 all-gather.10
  159.6 35.4 reduce-scatter.26
  198.0 26.2 all-gather.12
  259.8 35.4 reduce-scatter.28
  299.0 26.2 all-gather.14
  327.6 26.2 all-gather.16
  371.4 35.4 reduce-scatter.32
  415.4 26.3 all-gather.18
  484.1 35.4 reduce-scatter.34
  522.2 35.4 reduce-scatter.30
  562.4 26.2 all-gather.20
  606.5 35.4 reduce-scatter.36
  648.8 26.3 all-gather.22
  678.9 67.1 reduce-scatter.54
  750.2 61.4 reduce-scatter.50
  815.1 66.1 reduce-scatter.52
  884.9 66.7 reduce-scatter.46
  955.1 66.8 reduce-scatter.44
  1025.3 61.4 reduce-scatter.48
  1090.6 64.1 reduce-scatter.42
  1158.3 64.4 reduce-scatter.40
  1225.4 34.8 reduce-scatter.38
  1267.6 123.9 all-reduce.3
where the time goes:
time: 1420 us; the launch traced here: 1400 us
  waiting for transfers between devices  1030 us (73%)
  matrix products  164 us (12%)
  local copies, waits for them, and re-layouts  99.5 us (7%)
  other arithmetic  89.3 us (6%)
  between operations  16.6 us (1%)
    reduce_scatter x4, waiting for transfers between devices, collect_weight(): lax.psum_scatter(partial_grad.astype(jnp.bfloat16), 'dp', scatter_dimensi...  273 us
    unnamed x29, waiting for transfers between devices  203 us
    reduce_scatter x4, waiting for transfers between devices, collect(): lax.psum_scatter(partial_rows.astype(jnp.bfloat16), 'tensor', scatter_dim...  140 us
    reduce_scatter x4, waiting for transfers between devices, collect_grad(): lax.psum_scatter(partial_rows.astype(jnp.bfloat16), 'tensor', scatter_dim...  135 us
    psum x1, waiting for transfers between devices, local(): lax.psum((jnp.stack(gain_terms), jnp.stack(shift_terms), qv_full, fc1_ful...  122 us
    all_gather x4, waiting for transfers between devices, spread(): lax.all_gather(rows, 'tensor', axis=0, tiled=True)  96 us
    all_gather x4, waiting for transfers between devices, spread_grad(): return lax.all_gather(rows, 'tensor', axis=0, tiled=True)  58.4 us
    unnamed x219, local copies, waits for them, and re-layouts  41.5 us
  transfers between devices with their start and end apart: 25, of which 24 were waited for; matrix products, arithmetic and copies ran while one was open for 10% of the time, Pallas kernels for 0%

commit v1 on v0

--- a/solution.py
+++ b/solution.py
@@ -3,6 +3,7 @@
 import jax.numpy as jnp
 from jax import lax
 from jax.sharding import PartitionSpec as P
+from jax.lax import axis_index, ppermute, psum
 
 D = 1024
 HEAD = 64
@@ -13,6 +14,30 @@
 HIGHEST = lax.Precision.HIGHEST
 
 
+def meet_axis_part_on_mesh(arr, on_dim):
+    fresh = list(arr.shape[1:])
+    fresh[on_dim] *= arr.shape[0]
+    newest = jnp.moveaxis(arr, 0, on_dim).reshape(fresh)
+    return newest
+
+
+def _produce_links(my_tile, peer_axis):
+    f_now = psum(1, axis_name=peer_axis)
+    view_out = axis_index(peer_axis)
+    opened, seen_now = (f_now, view_out)
+    k_now, piece_next = (my_tile[None], 1)
+    while piece_next < opened:
+        response = ppermute(
+            k_now, axis_name=peer_axis, perm=[(q, q ^ piece_next) for q in range(opened)]
+        )
+        current_block = seen_now & piece_next == 0
+        moved = jnp.where(current_block, k_now, response)
+        big = jnp.where(current_block, response, k_now)
+        k_now = jnp.concatenate([moved, big])
+        piece_next *= 2
+    return k_now
+
+
 def norm_rows(values, scaling, offset):
     average = jnp.mean(values, axis=-1, keepdims=True)
     centred = values - average
@@ -34,7 +59,13 @@
 
 
 def spread_grad(rows):
-    return lax.all_gather(rows, "tensor", axis=0, tiled=True)
+
+    def step_on_slot(work_x, xin, where_dim):
+        carry_out = _produce_links(work_x, xin)
+        outer = meet_axis_part_on_mesh(carry_out, where_dim)
+        return outer
+
+    return step_on_slot(rows, xin="tensor", where_dim=0)
 
 
 def collect_grad(partial_rows):

time: 1420 us -> 1400 us (0.986)
    ppermute x0 -> x8, waiting for transfers between devices: none -> 136 us  [_produce_links(): ppermute(k_now, axis_name=peer_axis, perm=[(q, q ^ piece_next) for q in r...]
    all_gather x4 -> x0, waiting for transfers between devices: 58.4 us -> none  [spread_grad(): return lax.all_gather(rows, 'tensor', axis=0, tiled=True)]
    reduce_scatter x4, waiting for transfers between devices: 135 us -> 99.6 us  [collect_grad(): lax.psum_scatter(partial_rows.astype(jnp.bfloat16), 'tensor', scatter_dim...]
    unnamed x29 -> x25, waiting for transfers between devices: 203 us -> 170 us
    all_gather x4, waiting for transfers between devices: 96 us -> 73.1 us  [spread(): lax.all_gather(rows, 'tensor', axis=0, tiled=True)]
    unnamed x219 -> x237, local copies, waits for them, and re-layouts: 41.5 us -> 48.6 us
  transfers between devices with their start and end apart: 25 -> 29, of which waited for: 24 -> 26; matrix products, arithmetic and copies ran while one was open for 10% -> 9% of each run, Pallas kernels for 0% -> 0%
where the time goes in v1:
time: 1400 us; the launch traced here: 1390 us
  waiting for transfers between devices  1020 us (73%)
  matrix products  150 us (11%)
  local copies, waits for them, and re-layouts  109 us (8%)
  other arithmetic  86.3 us (6%)
  between operations  16.9 us (1%)
    reduce_scatter x4, waiting for transfers between devices, collect_weight(): lax.psum_scatter(partial_grad.astype(jnp.bfloat16), 'dp', scatter_dimensi...  272 us
    unnamed x25, waiting for transfers between devices  170 us
    reduce_scatter x4, waiting for transfers between devices, collect(): lax.psum_scatter(partial_rows.astype(jnp.bfloat16), 'tensor', scatter_dim...  141 us
    ppermute x8, waiting for transfers between devices, _produce_links(): ppermute(k_now, axis_name=peer_axis, perm=[(q, q ^ piece_next) for q in r...  136 us
    psum x1, waiting for transfers between devices, local(): lax.psum((jnp.stack(gain_terms), jnp.stack(shift_terms), qv_full, fc1_ful...  124 us
    reduce_scatter x4, waiting for transfers between devices, collect_grad(): lax.psum_scatter(partial_rows.astype(jnp.bfloat16), 'tensor', scatter_dim...  99.6 us
    all_gather x4, waiting for transfers between devices, spread(): lax.all_gather(rows, 'tensor', axis=0, tiled=True)  73.1 us
    unnamed x237, local copies, waits for them, and re-layouts  48.6 us
  transfers between devices with their start and end apart: 29, of which 26 were waited for; matrix products, arithmetic and copies ran while one was open for 9% of the time, Pallas kernels for 0%

profile of v1, /device:TPU:8, one launch (start us, length us, event | category | flops | bytes accessed | tf_op | source)
XLA Modules:
  0.0 1387.9 jit_solution(784194232037386536)
XLA Ops:
  13.4 4.9 all-reduce
  18.5 20.9 %all-gather.5.cloned.1.call-done = bf16[24,50,1024]{2,1,0:T(8,128)(2,1)} async-done(((bf16[6,50,1024]{2,1,0:T(8,128)(2,1)}), bf16[24,50,1024]{2,1,0:T(8,128)(2,1)}) %all-gather.5.cloned.1.call-update) | async-done | bytes 2457616 | tf_op jit(solution)/shard_map/all_gather | solution.py:50
  39.3 4.6 fusion.18
  68.3 35.6 %reduce-scatter.25.cloned.1.call-done = bf16[6,50,1024]{2,1,0:T(8,128)(2,1)} async-done(((bf16[24,50,1024]{2,1,0:T(8,128)(2,1)}), bf16[6,50,1024]{2,1,0:T(8,128)(2,1)}) %reduce-scatter.25.cloned.1.call-update) | async-done | bytes 614416 | tf_op jit(solution)/shard_map/reduce_scatter | solution.py:56
  107.0 26.2 %all-gather.7.cloned.1.call-done = bf16[24,50,1024]{2,1,0:T(8,128)(2,1)} async-done(((bf16[6,50,1024]{2,1,0:T(8,128)(2,1)}), bf16[24,50,1024]{2,1,0:T(8,128)(2,1)}) %all-gather.7.cloned.1.call-update) | async-done | bytes 2457616 | tf_op jit(solution)/shard_map/all_gather | solution.py:50
  133.2 7.1 convert_reduce_fusion.3
  140.3 13.4 multiply_convert_fusion.1
  155.2 4.4 convolution_convert_fusion.5
  159.7 35.6 %reduce-scatter.27.cloned.1.call-done = bf16[6,50,1024]{2,1,0:T(8,128)(2,1)} async-done(((bf16[24,50,1024]{2,1,0:T(8,128)(2,1)}), bf16[6,50,1024]{2,1,0:T(8,128)(2,1)}) %reduce-scatter.27.cloned.1.call-update) | async-done | bytes 614416 | tf_op jit(solution)/shard_map/reduce_scatter | solution.py:56
  198.6 26.0 %all-gather.9.cloned.1.call-done = bf16[24,50,1024]{2,1,0:T(8,128)(2,1)} async-done(((bf16[6,50,1024]{2,1,0:T(8,128)(2,1)}), bf16[24,50,1024]{2,1,0:T(8,128)(2,1)}) %all-gather.9.cloned.1.call-update) | async-done | bytes 2457616 | tf_op jit(solution)/shard_map/all_gather | solution.py:50
  224.6 4.6 fusion.14
  249.4 3.8 convolution_convert_fusion
  253.3 35.6 %reduce-scatter.29.cloned.1.call-done = bf16[6,50,1024]{2,1,0:T(8,128)(2,1)} async-done(((bf16[24,50,1024]{2,1,0:T(8,128)(2,1)}), bf16[6,50,1024]{2,1,0:T(8,128)(2,1)}) %reduce-scatter.29.cloned.1.call-update) | async-done | bytes 614416 | tf_op jit(solution)/shard_map/reduce_scatter | solution.py:56
  301.6 41.4 %collective-permute-done.1 = bf16[2,6,50,1024]{3,0,2,1:T(2,128)(2,1)} collective-permute-done((bf16[2,6,50,1024]{3,0,2,1:T(2,128)(2,1)}, bf16[2,6,50,1024]{3,0,2,1:T(2,128)(2,1)}, u32[]{:S(2)}, u32[]{:S(2)}) %collective-permute-start.1) | collective-permute-done | bytes 1228832 | tf_op jit(solution)/shard_map/ppermute | solution.py:30
  346.9 7.0 convert_reduce_fusion.1
  353.9 13.4 multiply_convert_fusion
  367.3 7.1 convert_reduce_fusion.4
  374.4 6.2 convolution_convert_fusion.3
  380.7 35.5 %reduce-scatter.33.cloned.1.call-done = bf16[6,50,1024]{2,1,0:T(8,128)(2,1)} async-done(((bf16[24,50,1024]{2,1,0:T(8,128)(2,1)}), bf16[6,50,1024]{2,1,0:T(8,128)(2,1)}) %reduce-scatter.33.cloned.1.call-update) | async-done | bytes 614416 | tf_op jit(solution)/shard_map/reduce_scatter | solution.py:72
  426.2 28.5 %collective-permute-done.3 = bf16[2,6,50,1024]{3,0,2,1:T(2,128)(2,1)S(1)} collective-permute-done((bf16[2,6,50,1024]{3,0,2,1:T(2,128)(2,1)S(1)}, bf16[2,6,50,1024]{3,0,2,1:T(2,128)(2,1)S(1)}, u32[]{:S(2)}, u32[]{:S(2)}) %collective-permute-start.3) | collective-permute-done | bytes 1228832 | tf_op jit(solution)/shard_map/ppermute | solution.py:30
  493.7 3.9 bitcast_convert_fusion.1
  497.7 7.0 convolution_convert_fusion.4
  504.7 28.6 %reduce-scatter.35.cloned.1.call-done = bf16[6,50,1024]{2,1,0:T(8,128)(2,1)} async-done(((bf16[24,50,1024]{2,1,0:T(8,128)(2,1)}), bf16[6,50,1024]{2,1,0:T(8,128)(2,1)}) %reduce-scatter.35.cloned.1.call-update) | async-done | bytes 614416 | tf_op jit(solution)/shard_map/reduce_scatter | solution.py:72
  536.7 34.7 %reduce-scatter.31.cloned.1.call-done = bf16[6,50,1024]{2,1,0:T(8,128)(2,1)} async-done(((bf16[24,50,1024]{2,1,0:T(8,128)(2,1)}), bf16[6,50,1024]{2,1,0:T(8,128)(2,1)}) %reduce-scatter.31.cloned.1.call-update) | async-done | bytes 614416 | tf_op jit(solution)/shard_map/reduce_scatter | solution.py:56
  571.4 4.1 convert_reduce_fusion.14
  580.0 28.5 %collective-permute-done.5 = bf16[2,6,50,1024]{3,0,2,1:T(2,128)(2,1)S(1)} collective-permute-done((bf16[2,6,50,1024]{3,0,2,1:T(2,128)(2,1)S(1)}, bf16[2,6,50,1024]{3,0,2,1:T(2,128)(2,1)S(1)}, u32[]{:S(2)}, u32[]{:S(2)}) %collective-permute-start.5) | collective-permute-done | bytes 1228832 | tf_op jit(solution)/shard_map/ppermute | solution.py:30
  612.2 6.0 convert_reduce_fusion.5
  619.8 4.5 convolution_convert_fusion.2
  626.0 6.5 bitcast_convert_fusion.2
  632.5 4.2 copy.174
  636.8 4.6 fusion.92
  643.6 6.8 bitcast_convert_fusion.3
  650.5 3.9 copy.172
  654.5 7.7 bitcast_convert_fusion.4
  662.3 6.4 bitcast_convert_fusion.5
  677.4 28.6 %collective-permute-done.7 = bf16[2,6,50,1024]{3,0,2,1:T(2,128)(2,1)S(1)} collective-permute-done((bf16[2,6,50,1024]{3,0,2,1:T(2,128)(2,1)S(1)}, bf16[2,6,50,1024]{3,0,2,1:T(2,128)(2,1)S(1)}, u32[]{:S(2)}, u32[]{:S(2)}) %collective-permute-start.7) | collective-permute-done | bytes 1228832 | tf_op jit(solution)/shard_map/ppermute | solution.py:30
  711.3 5.7 bitcast_convert_fusion.6
  743.9 3.8 bitcast_convert_fusion.7
  748.1 5.9 bitcast_convert_fusion
  755.9 40.7 %reduce-scatter.51.cloned.1.call-done = bf16[128,256]{1,0:T(8,128)(2,1)} async-done(((bf16[1024,256]{1,0:T(8,128)(2,1)}), bf16[128,256]{1,0:T(8,128)(2,1)}) %reduce-scatter.51.cloned.1.call-update) | async-done | bytes 65552
  797.6 68.3 %reduce-scatter.53.cloned.1.call-done = bf16[128,1024]{1,0:T(8,128)(2,1)} async-done(((bf16[1024,1024]{1,0:T(8,128)(2,1)}), bf16[128,1024]{1,0:T(8,128)(2,1)}) %reduce-scatter.53.cloned.1.call-update) | async-done | bytes 262160
  868.1 67.9 %reduce-scatter.47.cloned.1.call-done = bf16[128,1024]{1,0:T(8,128)(2,1)} async-done(((bf16[1024,1024]{1,0:T(8,128)(2,1)}), bf16[128,1024]{1,0:T(8,128)(2,1)}) %reduce-scatter.47.cloned.1.call-update) | async-done | bytes 262160 | tf_op jit(solution)/shard_map/reduce_scatter | solution.py:78
  936.0 70.1 %reduce-scatter.45.cloned.1.call-done = bf16[128,1024]{1,0:T(8,128)(2,1)} async-done(((bf16[1024,1024]{1,0:T(8,128)(2,1)}), bf16[128,1024]{1,0:T(8,128)(2,1)}) %reduce-scatter.45.cloned.1.call-update) | async-done | bytes 262160 | tf_op jit(solution)/shard_map/reduce_scatter | solution.py:78
  1009.8 61.1 %reduce-scatter.49.cloned.1.call-done = bf16[128,256]{1,0:T(8,128)(2,1)} async-done(((bf16[1024,256]{1,0:T(8,128)(2,1)}), bf16[128,256]{1,0:T(8,128)(2,1)}) %reduce-scatter.49.cloned.1.call-update) | async-done | bytes 65552
  1072.6 66.2 %reduce-scatter.43.cloned.1.call-done = bf16[128,3,256]{2,0,1:T(8,128)(2,1)} async-done(((bf16[1024,3,256]{2,0,1:T(8,128)(2,1)}), bf16[128,3,256]{2,0,1:T(8,128)(2,1)}) %reduce-scatter.43.cloned.1.call-update) | async-done | bytes 196624 | tf_op jit(solution)/shard_map/reduce_scatter | solution.py:78
  1138.8 67.9 %reduce-scatter.41.cloned.1.call-done = bf16[128,3,256]{2,0,1:T(8,128)(2,1)} async-done(((bf16[1024,3,256]{2,0,1:T(8,128)(2,1)}), bf16[128,3,256]{2,0,1:T(8,128)(2,1)}) %reduce-scatter.41.cloned.1.call-update) | async-done | bytes 196624 | tf_op jit(solution)/shard_map/reduce_scatter | solution.py:78
  1208.7 35.5 %reduce-scatter.39.cloned.1.call-done = bf16[6,50,1024]{2,1,0:T(8,128)(2,1)} async-done(((bf16[24,50,1024]{2,1,0:T(8,128)(2,1)}), bf16[6,50,1024]{2,1,0:T(8,128)(2,1)}) %reduce-scatter.39.cloned.1.call-update) | async-done | bytes 614416 | tf_op jit(solution)/shard_map/reduce_scatter | solution.py:72
  1251.5 124.0 %all-reduce.4.cloned.1.call-done = (f32[2,2,1024]{2,1,0:T(2,128)}, f32[2,4,1024]{2,1,0:T(4,128)}, f32[2,2,1024]{2,1,0:T(2,128)}, f32[2,4096]{1,0:T(2,128)}) async-done(((f32[2,2,1024]{2,1,0:T(2,128)}, f32[2,4,1024]{2,1,0:T(4,128)}, f32[2,2,1024]{2,1,0:T(2,128)}, f32[2,4096]{1,0:T(2,128)}), (f32[2,2,1024]{2,1,0:T(2,128)}, f32[2,4,1024]{2,1,0:T(4,128)}, f32[2,2,1024]{2,1,0:T(2,128)}, ...) | async-done | bytes 98320 | tf_op jit(solution)/shard_map/psum | solution.py:282
  (442 shorter events, 206.3 us)
Async XLA Ops:
  7.2 32.1 %all-gather.5.cloned.1.call-start = ((), (), s32[]{:S(2)}) async-start(), calls=%async_computation.16 | async-start | bytes 3440640 | tf_op jit(solution)/shard_map/all_gather | solution.py:50
  9.9 95.7 %copy-start.69 = (f32[1,1,1024]{2,1,0:T(1,128)}, f32[1,1,1024]{2,1,0:T(1,128)S(1)}, u32[]{:S(2)}) copy-start(f32[1,1,1024]{2,1,0:T(1,128)S(1)} %get-tuple-element.86) | copy-start | bytes 12292
  11.7 92.2 %reduce-scatter.25.cloned.1.call-start = ((), (), s32[]{:S(2)}) async-start(), calls=%async_computation.17 | async-start | bytes 3440640 | tf_op jit(solution)/shard_map/reduce_scatter | solution.py:56
  18.5 449.4 %copy-start.60 = (pred[24,50]{1,0:T(8,128)(4,1)}, pred[24,50]{1,0:T(8,128)(4,1)S(1)}, u32[]{:S(2)}) copy-start(pred[24,50]{1,0:T(8,128)(4,1)S(1)} %iota_compare_fusion.3) | copy-start | bytes 3604
  68.2 65.0 %all-gather.7.cloned.1.call-start = ((), (), s32[]{:S(2)}) async-start(), calls=%async_computation.18 | async-start | bytes 3440640 | tf_op jit(solution)/shard_map/all_gather | solution.py:50
  105.2 90.1 %copy-start.2 = (f32[6,50,1024]{2,1,0:T(8,128)}, f32[6,50,1024]{2,1,0:T(8,128)S(1)}, u32[]{:S(2)}) copy-start(f32[6,50,1024]{2,1,0:T(8,128)S(1)} %get-tuple-element.53) | copy-start | bytes 3686404
  106.7 88.5 %reduce-scatter.27.cloned.1.call-start = ((), (), s32[]{:S(2)}) async-start(), calls=%async_computation.19 | async-start | bytes 3440640 | tf_op jit(solution)/shard_map/reduce_scatter | solution.py:56
  159.7 64.9 %all-gather.9.cloned.1.call-start = ((), (), s32[]{:S(2)}) async-start(), calls=%async_computation.20 | async-start | bytes 3440640 | tf_op jit(solution)/shard_map/all_gather | solution.py:50
  198.1 90.7 %reduce-scatter.29.cloned.1.call-start = ((), (), s32[]{:S(2)}) async-start(), calls=%async_computation.21 | async-start | bytes 3440640 | tf_op jit(solution)/shard_map/reduce_scatter | solution.py:56
  253.2 93.6 %all-gather.11.cloned.1.call-start = ((), (), s32[]{:S(2)}) async-start(), calls=%async_computation.22 | async-start | bytes 3440640 | tf_op jit(solution)/shard_map/all_gather | solution.py:50
  291.7 124.5 %reduce-scatter.33.cloned.1.call-start = ((), (), s32[]{:S(2)}) async-start(), calls=%async_computation.24 | async-start | bytes 3440640 | tf_op jit(solution)/shard_map/reduce_scatter | solution.py:72
  293.9 2.5 collective-permute-start
  301.0 42.0 %collective-permute-start.1 = (bf16[2,6,50,1024]{3,0,2,1:T(2,128)(2,1)}, bf16[2,6,50,1024]{3,0,2,1:T(2,128)(2,1)}, u32[]{:S(2)}, u32[]{:S(2)}) collective-permute-start(bf16[2,6,50,1024]{3,0,2,1:T(2,128)(2,1)} %copy.109), channel_id=1, source_target_pairs={{0,2},{1,3},{2,0},{3,1},{4,6},{5,7},{6,4},{7,5},{8,10},{9,11},{10,... | collective-permute-start | bytes 3686408 | tf_op jit(solution)/shard_map/ppermute | solution.py:30
  380.6 152.7 %reduce-scatter.35.cloned.1.call-start = ((), (), s32[]{:S(2)}) async-start(), calls=%async_computation.25 | async-start | bytes 3440640 | tf_op jit(solution)/shard_map/reduce_scatter | solution.py:72
  421.9 2.1 collective-permute-start.2
  425.6 29.1 %collective-permute-start.3 = (bf16[2,6,50,1024]{3,0,2,1:T(2,128)(2,1)S(1)}, bf16[2,6,50,1024]{3,0,2,1:T(2,128)(2,1)S(1)}, u32[]{:S(2)}, u32[]{:S(2)}) collective-permute-start(bf16[2,6,50,1024]{3,0,2,1:T(2,128)(2,1)S(1)} %copy.112), channel_id=1, source_target_pairs={{0,2},{1,3},{2,0},{3,1},{4,6},{5,7},{6,4},{7,5},{8,10},{9,11},{10,... | collective-permute-start | bytes 3686408 | tf_op jit(solution)/shard_map/ppermute | solution.py:30
  497.6 73.7 %reduce-scatter.31.cloned.1.call-start = ((), (), s32[]{:S(2)}) async-start(), calls=%async_computation.23 | async-start | bytes 3440640 | tf_op jit(solution)/shard_map/reduce_scatter | solution.py:56
  504.7 164.1 %reduce-scatter.37.cloned.1.call-start = ((), (), s32[]{:S(2)}) async-start(), calls=%async_computation.26 | async-start | bytes 3440640 | tf_op jit(solution)/shard_map/reduce_scatter | solution.py:72
  575.6 2.2 collective-permute-start.4
  579.4 29.1 %collective-permute-start.5 = (bf16[2,6,50,1024]{3,0,2,1:T(2,128)(2,1)S(1)}, bf16[2,6,50,1024]{3,0,2,1:T(2,128)(2,1)S(1)}, u32[]{:S(2)}, u32[]{:S(2)}) collective-permute-start(bf16[2,6,50,1024]{3,0,2,1:T(2,128)(2,1)S(1)} %copy.128), channel_id=1, source_target_pairs={{0,2},{1,3},{2,0},{3,1},{4,6},{5,7},{6,4},{7,5},{8,10},{9,11},{10,... | collective-permute-start | bytes 3686408 | tf_op jit(solution)/shard_map/ppermute | solution.py:30
  624.3 129.8 %reduce-scatter.55.cloned.1.call-start = ((), (), s32[]{:S(2)}) async-start(), calls=%async_computation.35 | async-start | bytes 2359296
  636.8 159.8 %reduce-scatter.51.cloned.1.call-start = ((), (), s32[]{:S(2)}) async-start(), calls=%async_computation.33 | async-start | bytes 589824
  643.6 222.4 %reduce-scatter.53.cloned.1.call-start = ((), (), s32[]{:S(2)}) async-start(), calls=%async_computation.34 | async-start | bytes 2359296
  654.4 281.6 %reduce-scatter.47.cloned.1.call-start = ((), (), s32[]{:S(2)}) async-start(), calls=%async_computation.31 | async-start | bytes 2359296 | tf_op jit(solution)/shard_map/reduce_scatter | solution.py:78
  662.2 343.9 %reduce-scatter.45.cloned.1.call-start = ((), (), s32[]{:S(2)}) async-start(), calls=%async_computation.30 | async-start | bytes 2359296 | tf_op jit(solution)/shard_map/reduce_scatter | solution.py:78
  668.8 402.1 %reduce-scatter.49.cloned.1.call-start = ((), (), s32[]{:S(2)}) async-start(), calls=%async_computation.32 | async-start | bytes 589824
  673.0 2.2 collective-permute-start.6
  676.8 29.1 %collective-permute-start.7 = (bf16[2,6,50,1024]{3,0,2,1:T(2,128)(2,1)S(1)}, bf16[2,6,50,1024]{3,0,2,1:T(2,128)(2,1)S(1)}, u32[]{:S(2)}, u32[]{:S(2)}) collective-permute-start(bf16[2,6,50,1024]{3,0,2,1:T(2,128)(2,1)S(1)} %copy.131), channel_id=1, source_target_pairs={{0,2},{1,3},{2,0},{3,1},{4,6},{5,7},{6,4},{7,5},{8,10},{9,11},{10,... | collective-permute-start | bytes 3686408 | tf_op jit(solution)/shard_map/ppermute | solution.py:30
  711.2 427.6 %reduce-scatter.43.cloned.1.call-start = ((), (), s32[]{:S(2)}) async-start(), calls=%async_computation.29 | async-start | bytes 1769472 | tf_op jit(solution)/shard_map/reduce_scatter | solution.py:78
  717.0 489.7 %reduce-scatter.41.cloned.1.call-start = ((), (), s32[]{:S(2)}) async-start(), calls=%async_computation.28 | async-start | bytes 1769472 | tf_op jit(solution)/shard_map/reduce_scatter | solution.py:78
  747.8 496.4 %reduce-scatter.39.cloned.1.call-start = ((), (), s32[]{:S(2)}) async-start(), calls=%async_computation.27 | async-start | bytes 3440640 | tf_op jit(solution)/shard_map/reduce_scatter | solution.py:72
  754.0 43.6 %copy-start.92 = (f32[1024]{0:T(1024)S(1)}, f32[1024]{0:T(1024)}, u32[]{:S(2)}) copy-start(f32[1024]{0:T(1024)} %get-tuple-element.103) | copy-start | bytes 12292
  754.0 43.6 %copy-start.93 = (f32[1024]{0:T(1024)S(1)}, f32[1024]{0:T(1024)}, u32[]{:S(2)}) copy-start(f32[1024]{0:T(1024)} %get-tuple-element.105) | copy-start | bytes 12292
  754.0 621.5 %all-reduce.4.cloned.1.call-start = ((), (), s32[]{:S(2)}) async-start(), calls=%async_computation.36 | async-start | bytes 196608 | tf_op jit(solution)/shard_map/psum | solution.py:282
  797.6 212.2 %copy-start.66 = (f32[2,4096]{1,0:T(2,128)}, f32[2,4096]{1,0:T(2,128)S(1)}, u32[]{:S(2)}) copy-start(f32[2,4096]{1,0:T(2,128)S(1)} %maximum_dynamic-update-slice_fusion) | copy-start | bytes 98308
  868.1 376.1 %copy-start.6 = (f32[6,50,1024]{2,1,0:T(8,128)S(1)}, f32[6,50,1024]{2,1,0:T(8,128)}, u32[]{:S(2)}) copy-start(f32[6,50,1024]{2,1,0:T(8,128)} %copy-done.4) | copy-start | bytes 3686404
  868.1 376.1 %copy-start.63 = (f32[6,50]{1,0:T(8,128)S(1)}, f32[6,50]{1,0:T(8,128)}, u32[]{:S(2)}) copy-start(f32[6,50]{1,0:T(8,128)} %copy-done.62) | copy-start | bytes 3604
  868.1 376.1 %copy-start.68 = (f32[1,1,1024]{2,1,0:T(1,128)S(1)}, f32[1,1,1024]{2,1,0:T(1,128)}, u32[]{:S(2)}) copy-start(f32[1,1,1024]{2,1,0:T(1,128)} %copy-done.67) | copy-start | bytes 12292
  1008.2 237.6 %copy-start.77 = (f32[6,50]{1,0:T(8,128)S(1)}, f32[6,50]{1,0:T(8,128)}, u32[]{:S(2)}) copy-start(f32[6,50]{1,0:T(8,128)} %copy-done.76) | copy-start | bytes 3604
  1008.2 237.6 %copy-start.72 = (f32[6,50]{1,0:T(8,128)S(1)}, f32[6,50]{1,0:T(8,128)}, u32[]{:S(2)}) copy-start(f32[6,50]{1,0:T(8,128)} %copy-done.71) | copy-start | bytes 3604
  1009.8 236.7 %copy-start.75 = (f32[2,2,1024]{2,1,0:T(2,128)}, f32[2,2,1024]{2,1,0:T(2,128)S(1)}, u32[]{:S(2)}) copy-start(f32[2,2,1024]{2,1,0:T(2,128)S(1)} %maximum_dynamic-update-slice_fusion.1) | copy-start | bytes 49156
  1206.6 39.9 %copy-start.81 = (f32[1024]{0:T(1024)S(1)}, f32[1024]{0:T(1024)}, u32[]{:S(2)}) copy-start(f32[1024]{0:T(1024)} %get-tuple-element.40) | copy-start | bytes 12292
  1206.7 39.9 %copy-start.83 = (f32[1024]{0:T(1024)S(1)}, f32[1024]{0:T(1024)}, u32[]{:S(2)}) copy-start(f32[1024]{0:T(1024)} %get-tuple-element.75) | copy-start | bytes 12292
  1206.7 39.9 %copy-start.84 = (f32[1024]{0:T(1024)S(1)}, f32[1024]{0:T(1024)}, u32[]{:S(2)}) copy-start(f32[1024]{0:T(1024)} %get-tuple-element.28) | copy-start | bytes 12292
  1206.7 39.9 %copy-start.85 = (f32[1024]{0:T(1024)S(1)}, f32[1024]{0:T(1024)}, u32[]{:S(2)}) copy-start(f32[1024]{0:T(1024)} %get-tuple-element.42) | copy-start | bytes 12292
  1206.7 39.9 %copy-start.86 = (f32[1024]{0:T(1024)S(1)}, f32[1024]{0:T(1024)}, u32[]{:S(2)}) copy-start(f32[1024]{0:T(1024)} %get-tuple-element.26) | copy-start | bytes 12292
  1208.7 39.2 %copy-start.82 = (s32[6,50]{1,0:T(8,128)S(1)}, s32[6,50]{1,0:T(8,128)}, u32[]{:S(2)}) copy-start(s32[6,50]{1,0:T(8,128)} %param.13) | copy-start | bytes 3604
  1247.9 133.0 %copy-start.1 = (bf16[6,50,1024]{2,1,0:T(8,128)(2,1)S(1)}, bf16[6,50,1024]{2,1,0:T(8,128)(2,1)}, u32[]{:S(2)}) copy-start(bf16[6,50,1024]{2,1,0:T(8,128)(2,1)} %param.12) | copy-start | bytes 1843204
  (90 other events, 791.8 us)
Sparse Core Ops, SparseCore 0:
  11.8 27.4 all-gather.4
  68.4 35.4 reduce-scatter.24
  106.9 26.2 all-gather.6
  159.8 35.4 reduce-scatter.26
  198.3 26.2 all-gather.8
  253.3 35.4 reduce-scatter.28
  291.8 38.8 all-gather.10
  380.7 35.4 reduce-scatter.32
  497.8 35.4 reduce-scatter.34
  535.9 35.4 reduce-scatter.30
  624.4 35.4 reduce-scatter.36
  663.7 66.9 reduce-scatter.54
  735.0 61.5 reduce-scatter.50
  799.9 65.9 reduce-scatter.52
  869.3 66.6 reduce-scatter.46
  939.4 66.6 reduce-scatter.44
  1009.3 61.5 reduce-scatter.48
  1074.6 64.1 reduce-scatter.42
  1142.2 64.3 reduce-scatter.40
  1209.2 34.8 reduce-scatter.38
  1251.5 123.9 all-reduce.3
